TPU v7x, 32 devices: a whole 2x2x4 slice. The times are simulated.
32 devices in a mesh: sec: 4 (over y, core), ctx: 2 (over x), tp: 4 (over z).
Axes of the slice: x: 2, y: 2, z: 4, core: 2. Of those that a mesh axis runs over, the one named last changes fastest.
Arguments:
- self_query: bfloat16 [1024, 2048], P('ctx', ('sec', 'tp')), may hold values from -6 to 6
- self_key: bfloat16 [1024, 2048], P('ctx', ('sec', 'tp')), may hold values from -6 to 6
- self_value: bfloat16 [1024, 2048], P('ctx', ('sec', 'tp')), may hold values from -6 to 6
- self_gain: float32 [2048], P(('sec', 'tp')), may hold values from 0.5 to 1.5
- self_grad: bfloat16 [1024, 2048], P('ctx', ('sec', 'tp')), may hold values from -6 to 6
- cross_query: bfloat16 [1024, 2048], P('ctx', ('sec', 'tp')), may hold values from -6 to 6
- memory_key: bfloat16 [256, 2048], P(('sec', 'ctx')), may hold values from -6 to 6
- memory_value: bfloat16 [256, 2048], P(('sec', 'ctx')), may hold values from -6 to 6
- cross_gain: float32 [2048], P(('sec', 'tp')), may hold values from 0.5 to 1.5
- cross_grad: bfloat16 [1024, 2048], P('ctx', ('sec', 'tp')), may hold values from -6 to 6
- block_start: int32 [8], replicated, may hold values from 0 to 7, each once
Outputs:
- self_out: bfloat16 [1024, 2048], P('ctx', ('sec', 'tp'))
- cross_out: bfloat16 [1024, 2048], P('ctx', ('sec', 'tp'))
- query_grad: bfloat16 [1024, 2048], P('ctx', ('sec', 'tp'))
- key_grad: bfloat16 [1024, 2048], P('ctx', ('sec', 'tp'))
- value_grad: bfloat16 [1024, 2048], P('ctx', ('sec', 'tp'))
- cross_query_grad: bfloat16 [1024, 2048], P('ctx', ('sec', 'tp'))
- memory_key_grad: bfloat16 [256, 2048], P(('sec', 'ctx'))
- memory_value_grad: bfloat16 [256, 2048], P(('sec', 'ctx'))
Inputs may be any that keep to these rules, and one draw needn't show every extreme that they name: `block_start`: every number appears once.
All inputs are finite; a program needn't handle non-finite values.
Results may differ from a plain program's by a relative error of at most 0.015.
Values may be sent and summed in bfloat16 or wider, within the bound.
No kernel may reach another device: no remote copies, remote signals or barrier semaphores. Data moves between devices by JAX's collectives and lax.ppermute only.
A program may use at most 64 MiB of HBM per device.

v0:
```python
import math
import jax
import jax.numpy as jnp
from jax import lax
from jax.sharding import PartitionSpec as P

HEADS = 16
HEAD_DIM = 128
EPS = 1e-06
NEG_FILL = -1e30


def split_heads(matrix):
    return matrix.reshape(matrix.shape[0], matrix.shape[1] // HEAD_DIM, HEAD_DIM)


def frame_positions(block_start, first_row, row_count, block_rows):
    row_ids = first_row + jnp.arange(row_count, dtype=jnp.int32)
    owners = row_ids // block_rows
    lookup = owners[:, None] == jnp.arange(block_start.shape[0], dtype=jnp.int32)[None, :]
    starts = jnp.sum(jnp.where(lookup, block_start[None, :], 0), axis=1)
    return starts * block_rows + row_ids % block_rows


def skipped(key_positions, query_positions):
    return jnp.min(key_positions) > jnp.max(query_positions)


def masked_scores(queries, key_block, key_positions, query_positions, filler):
    scores = jnp.einsum("qhd,khd->hqk", queries, key_block, preferred_element_type=jnp.float32) * (
        1.0 / math.sqrt(HEAD_DIM)
    )
    if key_positions is None:
        return scores
    return jnp.where(key_positions[None, None, :] > query_positions[None, :, None], filler, scores)


def fold_softmax(carried, pieces, queries, query_positions, position_of):
    row_top, row_total, key_store, value_store = carried
    key_piece, value_piece = pieces
    row_count = key_piece.shape[0]
    key_store = key_piece
    value_store = value_piece
    block_length = math.gcd(row_count, 1024)

    def fold_visit(turn_index, running):
        offset = turn_index * block_length
        key_block = split_heads(lax.dynamic_slice_in_dim(key_piece, offset, block_length, 0))
        key_positions = None if position_of is None else position_of(offset, block_length)

        def update(current):
            old_top, old_total = current
            scores = masked_scores(queries, key_block, key_positions, query_positions, NEG_FILL)
            new_top = jnp.maximum(old_top, jnp.max(scores, axis=2))
            new_total = old_total * jnp.exp(old_top - new_top) + jnp.sum(
                jnp.exp(scores - new_top[:, :, None]), axis=2
            )
            return (new_top, new_total)

        if key_positions is None:
            return update(running)
        return lax.cond(
            skipped(key_positions, query_positions), lambda unused: unused, update, running
        )

    row_top, row_total = lax.fori_loop(
        0, row_count // block_length, fold_visit, (row_top, row_total)
    )
    return (row_top, row_total, key_store, value_store)


def attend(queries, log_total, key_store, value_store, query_positions, position_of):
    key_count = key_store.shape[0]
    block_length = math.gcd(key_count, 512)

    def attend_visit(turn_index, running):
        offset = turn_index * block_length
        key_block = split_heads(lax.dynamic_slice_in_dim(key_store, offset, block_length, 0))
        value_block = split_heads(lax.dynamic_slice_in_dim(value_store, offset, block_length, 0))
        key_positions = None if position_of is None else position_of(offset, block_length)

        def update(current):
            scores = masked_scores(queries, key_block, key_positions, query_positions, -jnp.inf)
            weights = jnp.exp(scores - log_total[:, :, None]).astype(jnp.bfloat16)
            return current + jnp.einsum(
                "hqk,khd->qhd", weights, value_block, preferred_element_type=jnp.float32
            )

        if key_positions is None:
            return update(running)
        return lax.cond(
            skipped(key_positions, query_positions), lambda unused: unused, update, running
        )

    result = lax.fori_loop(
        0, key_count // block_length, attend_visit, jnp.zeros(queries.shape, jnp.float32)
    )
    return result.reshape(queries.shape[0], queries.shape[1] * HEAD_DIM)


def score_parts(
    queries, cotangent, log_total, row_delta, key_block, value_block, key_positions, query_positions
):
    scores = masked_scores(queries, key_block, key_positions, query_positions, -jnp.inf)
    weights = jnp.exp(scores - log_total[:, :, None])
    products = jnp.einsum(
        "qhd,khd->hqk", cotangent, value_block, preferred_element_type=jnp.float32
    )
    score_grad = (weights * (products - row_delta[:, :, None])).astype(jnp.bfloat16)
    return (weights, score_grad)


def key_side_terms(queries, cotangent, weights, score_grad):
    key_part = jnp.einsum(
        "hqk,qhd->khd", score_grad, queries, preferred_element_type=jnp.float32
    ) * (1.0 / math.sqrt(HEAD_DIM))
    value_part = jnp.einsum(
        "hqk,qhd->khd", weights.astype(jnp.bfloat16), cotangent, preferred_element_type=jnp.float32
    )
    rows_here = key_part.shape[0]
    return jnp.concatenate(
        [key_part.reshape(rows_here, -1), value_part.reshape(rows_here, -1)], axis=1
    )


def joint_backward(
    queries, cotangent, log_total, row_delta, key_store, value_store, query_positions, position_of
):
    key_count = key_store.shape[0]
    block_length = math.gcd(key_count, 512)
    columns = queries.shape[1] * HEAD_DIM

    def joint_visit(turn_index, running):
        offset = turn_index * block_length
        key_block = split_heads(lax.dynamic_slice_in_dim(key_store, offset, block_length, 0))
        value_block = split_heads(lax.dynamic_slice_in_dim(value_store, offset, block_length, 0))
        key_positions = None if position_of is None else position_of(offset, block_length)

        def update(current):
            query_sum, key_terms = current
            weights, score_grad = score_parts(
                queries,
                cotangent,
                log_total,
                row_delta,
                key_block,
                value_block,
                key_positions,
                query_positions,
            )
            query_sum = query_sum + jnp.einsum(
                "hqk,khd->qhd", score_grad, key_block, preferred_element_type=jnp.float32
            ) * (1.0 / math.sqrt(HEAD_DIM))
            key_terms = lax.dynamic_update_slice_in_dim(
                key_terms, key_side_terms(queries, cotangent, weights, score_grad), offset, 0
            )
            return (query_sum, key_terms)

        if key_positions is None:
            return update(running)
        return lax.cond(
            skipped(key_positions, query_positions), lambda unused: unused, update, running
        )

    start_value = (
        jnp.zeros(queries.shape, jnp.float32),
        jnp.zeros((key_count, 2 * columns), jnp.float32),
    )
    query_sum, key_terms = lax.fori_loop(0, key_count // block_length, joint_visit, start_value)
    return (query_sum.reshape(queries.shape[0], columns), key_terms)


def backprop_norm(attended, lifted, row_scale, row_slope):
    return (
        row_scale[:, None] * (lifted - attended * (row_scale * row_scale * row_slope)[:, None])
    ).astype(jnp.bfloat16)


def head_delta(attended_grad, attended):
    return jnp.sum(
        (attended_grad.astype(jnp.float32) * attended).reshape(attended.shape[0], -1, HEAD_DIM),
        axis=2,
    ).T


def per_device(
    self_query,
    self_key,
    self_value,
    self_gain,
    self_grad,
    cross_query,
    memory_key,
    memory_value,
    cross_gain,
    cross_grad,
    block_start,
):
    frames_dev, columns = self_query.shape
    quarter_rows = frames_dev // 4
    full_width = HEADS * HEAD_DIM
    context_count = lax.axis_size("ctx")
    section_count = lax.axis_size("sec")
    tensor_count = lax.axis_size("tp")
    memory_rows = memory_key.shape[0]
    head_count = columns // HEAD_DIM
    own_positions = frame_positions(
        block_start, lax.axis_index("ctx") * frames_dev, frames_dev, quarter_rows
    )

    def position_of(first_row, row_count):
        return frame_positions(block_start, first_row, row_count, quarter_rows)

    own_queries = split_heads(self_query)
    empty_top = jnp.full((head_count, frames_dev), NEG_FILL, jnp.float32)
    empty_total = jnp.zeros((head_count, frames_dev), jnp.float32)
    frame_store = jnp.zeros((frames_dev * context_count, columns), jnp.bfloat16)
    self_top, self_sum, key_store, value_store = fold_softmax(
        (empty_top, empty_total, frame_store, frame_store),
        (
            lax.all_gather(self_key, "ctx", axis=0, tiled=True),
            lax.all_gather(self_value, "ctx", axis=0, tiled=True),
        ),
        own_queries,
        own_positions,
        position_of,
    )
    self_log_total = self_top + jnp.log(self_sum)
    self_attended = attend(
        own_queries, self_log_total, key_store, value_store, own_positions, position_of
    )

    def own_heads(memory):
        grouped = memory.reshape(memory_rows, section_count, tensor_count, columns)
        picked = lax.dynamic_slice_in_dim(grouped, lax.axis_index("tp"), 1, 2)
        return picked.reshape(memory_rows, section_count, columns)

    memory_keys, memory_values = (
        lax.all_to_all(own_heads(memory_key), "sec", split_axis=1, concat_axis=0, tiled=True),
        lax.all_to_all(own_heads(memory_value), "sec", split_axis=1, concat_axis=0, tiled=True),
    )
    section_rows = section_count * memory_rows
    memory_keys = memory_keys.reshape(section_rows, columns)
    memory_values = memory_values.reshape(section_rows, columns)
    cross_queries = split_heads(cross_query)
    memory_store = jnp.zeros((section_rows * context_count, columns), jnp.bfloat16)
    cross_top, cross_sum, memory_key_store, memory_value_store = fold_softmax(
        (empty_top, empty_total, memory_store, memory_store),
        (
            lax.all_gather(memory_keys, "ctx", axis=0, tiled=True),
            lax.all_gather(memory_values, "ctx", axis=0, tiled=True),
        ),
        cross_queries,
        own_positions,
        None,
    )
    cross_log_total = cross_top + jnp.log(cross_sum)
    cross_attended = attend(
        cross_queries, cross_log_total, memory_key_store, memory_value_store, own_positions, None
    )
    self_lifted = self_gain[None, :] * self_grad.astype(jnp.float32)
    cross_lifted = cross_gain[None, :] * cross_grad.astype(jnp.float32)
    self_squares = jnp.sum(self_attended * self_attended, axis=1)
    cross_squares = jnp.sum(cross_attended * cross_attended, axis=1)
    self_square_sum, cross_square_sum = lax.psum((self_squares, cross_squares), ("sec", "tp"))
    self_scale = lax.rsqrt(self_square_sum / full_width + EPS)
    cross_scale = lax.rsqrt(cross_square_sum / full_width + EPS)
    self_out = (self_gain[None, :] * self_attended * self_scale[:, None]).astype(jnp.bfloat16)
    cross_out = (cross_gain[None, :] * cross_attended * cross_scale[:, None]).astype(jnp.bfloat16)
    self_slope_sum, cross_slope_sum = lax.psum(
        (
            jnp.sum(self_lifted * self_attended, axis=1),
            jnp.sum(cross_lifted * cross_attended, axis=1),
        ),
        ("sec", "tp"),
    )
    self_attended_grad = backprop_norm(
        self_attended, self_lifted, self_scale, self_slope_sum / full_width
    )
    cross_attended_grad = backprop_norm(
        cross_attended, cross_lifted, cross_scale, cross_slope_sum / full_width
    )
    self_delta = head_delta(self_attended_grad, self_attended)
    self_cotangent = split_heads(self_attended_grad)
    query_sum, all_terms = joint_backward(
        own_queries,
        self_cotangent,
        self_log_total,
        self_delta,
        key_store,
        value_store,
        own_positions,
        position_of,
    )
    query_grad = query_sum.astype(jnp.bfloat16)
    key_terms = lax.psum_scatter(
        all_terms.astype(jnp.bfloat16), "ctx", scatter_dimension=0, tiled=True
    ).astype(jnp.float32)
    key_grad = key_terms[:, :columns].astype(jnp.bfloat16)
    value_grad = key_terms[:, columns:].astype(jnp.bfloat16)
    cross_delta = head_delta(cross_attended_grad, cross_attended)
    cross_query_sum, memory_terms = joint_backward(
        cross_queries,
        split_heads(cross_attended_grad),
        cross_log_total,
        cross_delta,
        memory_key_store,
        memory_value_store,
        None,
        None,
    )
    cross_query_grad = cross_query_sum.astype(jnp.bfloat16)
    memory_sums = lax.psum_scatter(
        memory_terms.astype(jnp.bfloat16), "ctx", scatter_dimension=0, tiled=True
    )
    rounded = memory_sums.reshape(section_rows, 2, 1, 1, columns)
    returned = lax.all_to_all(rounded, "sec", split_axis=0, concat_axis=2, tiled=True)
    complete = lax.all_gather(returned, "tp", axis=3, tiled=True).reshape(
        memory_rows, 2, section_count * tensor_count * columns
    )
    return (
        self_out,
        cross_out,
        query_grad,
        key_grad,
        value_grad,
        cross_query_grad,
        complete[:, 0],
        complete[:, 1],
    )


def solution(mesh):
    return jax.shard_map(
        per_device,
        mesh=mesh,
        in_specs=(
            P("ctx", ("sec", "tp")),
            P("ctx", ("sec", "tp")),
            P("ctx", ("sec", "tp")),
            P(("sec", "tp")),
            P("ctx", ("sec", "tp")),
            P("ctx", ("sec", "tp")),
            P(("sec", "ctx"), None),
            P(("sec", "ctx"), None),
            P(("sec", "tp")),
            P("ctx", ("sec", "tp")),
            P(),
        ),
        out_specs=(
            P("ctx", ("sec", "tp")),
            P("ctx", ("sec", "tp")),
            P("ctx", ("sec", "tp")),
            P("ctx", ("sec", "tp")),
            P("ctx", ("sec", "tp")),
            P("ctx", ("sec", "tp")),
            P(("sec", "ctx"), None),
            P(("sec", "ctx"), None),
        ),
        check_vma=False,
    )
```

profile of v0, /device:TPU:0, one launch (start us, length us, event | category | flops | bytes accessed | tf_op | source)
XLA Modules:
  0.0 131.9 jit_solution(3163522244689246081)
XLA Ops:
  7.2 1.0 reshape.417
  8.3 0.6 copy.78
  8.9 4.3 %all-to-all-start.1 = ((bf16[32,4,128]{2,0,1:T(8,128)(2,1)}), bf16[32,4,128]{2,0,1:T(8,128)(2,1)S(1)}, u32[]{:S(2)}, u32[]{:S(2)}) async-start(bf16[32,4,128]{2,0,1:T(8,128)(2,1)} %bitcast.165), calls=%async_computation.1 | async-start | bytes 65536 | tf_op jit(solution)/shard_map/all_to_all | solution.py:239
  13.2 1.0 reshape.414
  14.2 0.7 select_reduce_fusion.3
  14.9 0.6 fusion.88
  15.6 7.0 %all_gather.16 = bf16[1024,128]{1,0:T(8,128)(2,1)S(1)} all-gather(bf16[512,128]{1,0:T(8,128)(2,1)} %param.22), channel_id=1, replica_groups=mesh['sec'=4,'ctx'=2,'tp'=4] {'ctx'}, dimensions={0}, use_global_device_ids=true | all-gather | bytes 393216 | tf_op jit(solution)/shard_map/all_gather | solution.py:221
  22.6 0.7 select_reduce_fusion.2
  23.3 0.6 fusion.86
  25.3 6.2 %all_gather.15 = bf16[1024,128]{1,0:T(8,128)(2,1)S(1)} all-gather(bf16[512,128]{1,0:T(8,128)(2,1)} %param.23), channel_id=1, replica_groups=mesh['sec'=4,'ctx'=2,'tp'=4] {'ctx'}, dimensions={0}, use_global_device_ids=true | all-gather | bytes 393216 | tf_op jit(solution)/shard_map/all_gather | solution.py:222
  31.4 2.2 %conditional.3 = (f32[1,512]{1,0:T(1,128)S(1)}, f32[1,512]{1,0:T(1,128)S(1)}) conditional(s32[]{:T(128)} %convert_element_type.106, (s32[1024]{0:T(1024)S(1)}, s32[512]{0:T(512)S(1)}, bf16[512,1,128]{2,0,1:T(8,128)(2,1)}, bf16[1024,128]{1,0:T(8,128)(2,1)S(1)}, f32[1,512]{1,0:T(1,128)S(1)}, /*index=5*/f32[1,512]{1,0:T(1,128)S(1)}) %tuple.182, ...), branch_computations={%region_4.7_spmd, %region_7.8_spmd} | conditional | flops 138937344 | bytes 4622352 | solution.py:62
  31.4 1.5 %fusion = (f32[512]{0:T(512)S(1)}, f32[512,1024]{1,0:T(8,128)S(1)}) fusion(s32[1024]{0:T(1024)S(1)} %get-tuple-element.800, s32[512]{0:T(512)S(1)} %get-tuple-element.801, bf16[1024,128]{1,0:T(8,128)(2,1)S(1)} %get-tuple-element.803, bf16[512,1,128]{2,0,1:T(8,128)(2,1)} %get-tuple-element.802), kind=kOutput, calls=%fused_computation.2 | convolution fusion | flops 136314368 | bytes 2498560 | tf_op jit(solution)/shard_map/while/body/eval_jaxpr/cond/branch_0_fun/qhd,khd->hqk/dot_general | solution.py:30
  32.9 0.7 exponential_reduce_fusion
  33.7 7.2 %while.24 = (s32[]{:T(128)}, f32[512,1,128]{0,2,1:T(8,128)S(1)}, s32[8]{0:T(128)S(1)}, s32[]{:T(128)}, bf16[1024,128]{1,0:T(8,128)(2,1)S(1)}, /*index=5*/s32[512...) while((s32[]{:T(128)}, f32[512,1,128]{0,2,1:T(8,128)S(1)}, ...), condition=%wide.region_13.14_spmd, body=%wide.region_8.13_spmd.sunk | while | flops 135621632 | bytes 935197 | solution.py:95
  33.8 0.6 fusion.107
  35.7 1.5 %conditional.6 = (f32[512,1,128]{0,2,1:T(8,128)S(1)}) conditional(s32[]{:T(128)} %convert_element_type.172, (s32[]{:T(128)}, bf16[1024,128]{1,0:T(8,128)(2,1)S(1)}, s32[512]{0:T(512)S(1)}, s32[512]{0:T(512)S(1)}, bf16[1024,128]{1,0:T(8,128)(2,1)S(1)}, /*index=5*/bf16[512,1,128]{2,0,1:T(8,128)(2,1)}, f32[1,512]{1,0:T(1,128)S(1)}, ...), branch_computations={%region_11.11_spmd, %region_12.12_spmd} | conditional | flops 135593984 | bytes 924714 | solution.py:91
  35.8 1.5 %fusion.10 = f32[512,1,128]{0,2,1:T(8,128)S(1)} fusion(f32[512,1,128]{0,2,1:T(8,128)S(1)} %get-tuple-element.807, f32[512]{0:T(512)S(1)} %bitcast.178, s32[512]{0:T(512)S(1)} %get-tuple-element.811, s32[512]{0:T(512)S(1)} %get-tuple-element.810, bf16[512,1,128]{2,0,1:T(8,128)(2,1)} %get-tuple-element.813, bf16[1024,128]{1,0:T(8,128)(2,1)S(1)} %get-tuple-element.812, ...), kind=kOutput, calls=%fused_computation.14 | convolution fusion | flops 135593984 | bytes 924672 | tf_op jit(solution)/shard_map/while/body/eval_jaxpr/cond/branch_0_fun/hqk,khd->qhd/dot_general | solution.py:85
  37.4 0.6 fusion.107
  39.3 1.5 %conditional.6 = (f32[512,1,128]{0,2,1:T(8,128)S(1)}) conditional(s32[]{:T(128)} %convert_element_type.172, (s32[]{:T(128)}, bf16[1024,128]{1,0:T(8,128)(2,1)S(1)}, s32[512]{0:T(512)S(1)}, s32[512]{0:T(512)S(1)}, bf16[1024,128]{1,0:T(8,128)(2,1)S(1)}, /*index=5*/bf16[512,1,128]{2,0,1:T(8,128)(2,1)}, f32[1,512]{1,0:T(1,128)S(1)}, ...), branch_computations={%region_11.11_spmd, %region_12.12_spmd} | conditional | flops 135593984 | bytes 924714 | solution.py:91
  39.3 1.5 %fusion.10 = f32[512,1,128]{0,2,1:T(8,128)S(1)} fusion(f32[512,1,128]{0,2,1:T(8,128)S(1)} %get-tuple-element.807, f32[512]{0:T(512)S(1)} %bitcast.178, s32[512]{0:T(512)S(1)} %get-tuple-element.811, s32[512]{0:T(512)S(1)} %get-tuple-element.810, bf16[512,1,128]{2,0,1:T(8,128)(2,1)} %get-tuple-element.813, bf16[1024,128]{1,0:T(8,128)(2,1)S(1)} %get-tuple-element.812, ...), kind=kOutput, calls=%fused_computation.14 | convolution fusion | flops 135593984 | bytes 924672 | tf_op jit(solution)/shard_map/while/body/eval_jaxpr/cond/branch_0_fun/hqk,khd->qhd/dot_general | solution.py:85
  40.9 0.1 copy.60
  41.0 0.2 fusion.64
  41.3 0.6 copy.79
  42.1 3.3 %all-to-all-start = ((bf16[32,4,128]{2,0,1:T(8,128)(2,1)}), bf16[32,4,128]{2,0,1:T(8,128)(2,1)S(1)}, u32[]{:S(2)}, u32[]{:S(2)}) async-start(bf16[32,4,128]{2,0,1:T(8,128)(2,1)} %bitcast.166), calls=%async_computation | async-start | bytes 65536 | tf_op jit(solution)/shard_map/all_to_all | solution.py:240
  45.4 4.6 %all_gather.18 = bf16[256,128]{1,0:T(8,128)(2,1)S(1)} all-gather(bf16[128,128]{1,0:T(8,128)(2,1)S(1)} %bitcast.172), channel_id=1, replica_groups=mesh['sec'=4,'ctx'=2,'tp'=4] {'ctx'}, dimensions={0}, use_global_device_ids=true | all-gather | bytes 98304 | tf_op jit(solution)/shard_map/all_gather | solution.py:250
  50.0 0.2 fusion.91
  50.4 4.6 %all_gather.17 = bf16[256,128]{1,0:T(8,128)(2,1)S(1)} all-gather(bf16[128,128]{1,0:T(8,128)(2,1)S(1)} %bitcast.173), channel_id=1, replica_groups=mesh['sec'=4,'ctx'=2,'tp'=4] {'ctx'}, dimensions={0}, use_global_device_ids=true | all-gather | bytes 98304 | tf_op jit(solution)/shard_map/all_gather | solution.py:251
  55.0 0.3 multiply_reduce_fusion.1
  55.2 32.7 %all-reduce = (f32[512]{0:T(512)S(1)}, f32[512]{0:T(512)S(1)}, f32[512]{0:T(512)S(1)}, f32[512]{0:T(512)S(1)}) all-reduce(f32[512]{0:T(512)S(1)} %get-tuple-element.924, f32[512]{0:T(512)S(1)} %get-tuple-element.922, f32[512]{0:T(512)S(1)} %get-tuple-element.923, ...), channel_id=1, replica_groups=mesh['sec'=4,'ctx'=2,'tp'=4] {'sec','tp'}, use_global_device_ids=true, to_apply=%region_15.16 | all-reduce | flops 2048 | bytes 16384 | tf_op jit(solution)/shard_map/psum | solution.py:265
  88.0 0.2 multiply_reduce_fusion
  88.2 0.2 fusion.60
  88.4 0.2 fusion.56
  88.6 0.2 fusion.59
  88.9 0.8 copy.74
  89.7 0.9 fusion.68
  90.7 7.5 %while.25 = (s32[]{:T(128)}, f32[512,1,128]{0,2,1:T(8,128)S(1)}, bf16[1024,256]{0,1:T(8,128)(2,1)S(1)}, s32[8]{0:T(128)S(1)}, s32[]{:T(128)}, /*index=5*/bf16[10...) while((s32[]{:T(128)}, f32[512,1,128]{0,2,1:T(8,128)S(1)}, ...), condition=%wide.region_28.29_spmd, body=%wide.region_23.28_spmd.sunk | while | flops 338455552 | bytes 6965629 | solution.py:169
  90.8 0.6 fusion.108
  92.7 1.7 %conditional.7 = ((f32[512,1,128]{0,2,1:T(8,128)S(1)}, bf16[1024,256]{0,1:T(8,128)(2,1)S(1)})) conditional(s32[]{:T(128)} %convert_element_type.173, (s32[]{:T(128)}, bf16[1024,128]{1,0:T(8,128)(2,1)S(1)}, s32[512]{0:T(512)S(1)}, s32[512]{0:T(512)S(1)}, bf16[512,1,128]{2,0,1:T(8,128)(2,1)S(1)}, /*index=5*/f32[1,512]{1,0:T(1,128)S(1)}, ...), branch_computations={%region_26.26_spmd, %region_27.27_spmd} | conditional | flops 338427904 | bytes 6955082 | solution.py:161
  92.8 0.4 fusion.35
  93.2 0.3 fusion.36
  93.5 0.3 convolution_multiply_fusion.2
  93.8 0.3 fusion.39
  94.1 0.3 fusion.38
  94.6 0.6 fusion.108
  96.5 1.7 %conditional.7 = ((f32[512,1,128]{0,2,1:T(8,128)S(1)}, bf16[1024,256]{0,1:T(8,128)(2,1)S(1)})) conditional(s32[]{:T(128)} %convert_element_type.173, (s32[]{:T(128)}, bf16[1024,128]{1,0:T(8,128)(2,1)S(1)}, s32[512]{0:T(512)S(1)}, s32[512]{0:T(512)S(1)}, bf16[512,1,128]{2,0,1:T(8,128)(2,1)S(1)}, /*index=5*/f32[1,512]{1,0:T(1,128)S(1)}, ...), branch_computations={%region_26.26_spmd, %region_27.27_spmd} | conditional | flops 338427904 | bytes 6955082 | solution.py:161
  96.5 0.4 fusion.35
  96.9 0.3 fusion.36
  97.2 0.3 convolution_multiply_fusion.2
  97.5 0.3 fusion.39
  97.9 0.3 fusion.38
  98.2 1.0 copy.64
  99.2 0.9 copy.75
  100.2 0.8 copy.67
  101.0 3.3 %all-to-all-start.2 = ((bf16[128,2,1,1,128]{4,1,3,2,0:T(2,128)(2,1)}), bf16[128,2,1,1,128]{4,1,3,2,0:T(2,128)(2,1)S(1)}, u32[]{:S(2)}, u32[]{:S(2)}) async-start(bf16[128,2,1,1,128]{4,1,3,2,0:T(2,128)(2,1)} %copy.67), calls=%async_computation.3 | async-start | bytes 131072 | tf_op jit(solution)/shard_map/all_to_all | solution.py:317
  104.3 0.2 fusion.58
  104.5 0.8 copy.72
  105.2 0.8 copy.63
  106.0 0.8 copy.71
  106.8 1.6 %all-to-all-done.2 = bf16[128,2,1,1,128]{4,1,3,2,0:T(2,128)(2,1)S(1)} async-done(((bf16[128,2,1,1,128]{4,1,3,2,0:T(2,128)(2,1)}), bf16[128,2,1,1,128]{4,1,3,2,0:T(2,128)(2,1)S(1)}, u32[]{:S(2)}, u32[]{:S(2)}) %all-to-all-start.2) | async-done | bytes 65568 | tf_op jit(solution)/shard_map/all_to_all | solution.py:317
  108.4 13.9 %all-gather = bf16[32,2,4,4,1,128]{5,0,4,2,1,3:T(8,128)(2,1)S(1)} all-gather(bf16[32,2,4,1,1,128]{5,0,4,2,1,3:T(8,128)(2,1)S(1)} %bitcast.169), channel_id=2, replica_groups=mesh['sec'=4,'ctx'=2,'tp'=4] {'tp'}, dimensions={3}, use_global_device_ids=true | all-gather | bytes 327680 | tf_op jit(solution)/shard_map/all_gather | solution.py:318
  122.2 0.2 copy.70
  122.4 0.2 reshape.424
  122.6 0.7 slice_bitcast_fusion
  123.3 1.7 %fusion.90 = (bf16[512,128]{1,0:T(8,128)(2,1)}, bf16[512,128]{1,0:T(8,128)(2,1)}) fusion(bf16[512,256]{1,0:T(8,128)(2,1)} %reduce-scatter.5.cloned.1.call-done), kind=kLoop, calls=%fused_computation.160 | loop fusion | bytes 524288 | tf_op jit(solution)/shard_map/slice | solution.py:300
  (51 shorter events, 1.2 us)
Async XLA Ops:
  7.2 42.8 %copy-start = (bf16[512,128]{1,0:T(8,128)(2,1)S(1)}, bf16[512,128]{1,0:T(8,128)(2,1)}, u32[]{:S(2)}) copy-start(bf16[512,128]{1,0:T(8,128)(2,1)} %param.26) | copy-start | bytes 393220
  8.9 33.2 %all-to-all-start.1 = ((bf16[32,4,128]{2,0,1:T(8,128)(2,1)}), bf16[32,4,128]{2,0,1:T(8,128)(2,1)S(1)}, u32[]{:S(2)}, u32[]{:S(2)}) async-start(bf16[32,4,128]{2,0,1:T(8,128)(2,1)} %bitcast.165), calls=%async_computation.1 | async-start | bytes 65536 | tf_op jit(solution)/shard_map/all_to_all | solution.py:239
  31.4 2.2 %copy-start.4 = (s32[8]{0:T(128)S(1)}, s32[8]{0:T(128)}, u32[]{:S(2)}) copy-start(s32[8]{0:T(128)} %param.31) | copy-start | bytes 100
  33.6 7.4 %copy-start.2 = (bf16[512,128]{1,0:T(8,128)(2,1)S(1)}, bf16[512,128]{1,0:T(8,128)(2,1)}, u32[]{:S(2)}) copy-start(bf16[512,128]{1,0:T(8,128)(2,1)} %param.25) | copy-start | bytes 393220
  33.6 7.4 %copy-start.6 = (f32[128]{0:T(128)S(1)}, f32[128]{0:T(128)}, u32[]{:S(2)}) copy-start(f32[128]{0:T(128)} %param.24) | copy-start | bytes 1540
  33.7 8.3 %copy-start.3 = (bf16[512,128]{1,0:T(8,128)(2,1)S(1)}, bf16[512,128]{1,0:T(8,128)(2,1)}, u32[]{:S(2)}) copy-start(bf16[512,128]{1,0:T(8,128)(2,1)} %param.30) | copy-start | bytes 393220
  40.9 14.1 %copy-start.5 = (f32[128]{0:T(128)S(1)}, f32[128]{0:T(128)}, u32[]{:S(2)}) copy-start(f32[128]{0:T(128)} %param.29) | copy-start | bytes 1540
  42.1 8.3 %all-to-all-start = ((bf16[32,4,128]{2,0,1:T(8,128)(2,1)}), bf16[32,4,128]{2,0,1:T(8,128)(2,1)S(1)}, u32[]{:S(2)}, u32[]{:S(2)}) async-start(bf16[32,4,128]{2,0,1:T(8,128)(2,1)} %bitcast.166), calls=%async_computation | async-start | bytes 65536 | tf_op jit(solution)/shard_map/all_to_all | solution.py:240
  45.4 53.9 %reduce-scatter.7.cloned.1.call-start = ((), (), s32[]{:S(2)}) async-start(), calls=%async_computation.6 | async-start | bytes 196608
  88.1 2.5 %copy-start.1 = (bf16[512,1,128]{2,0,1:T(8,128)(2,1)S(1)}, bf16[512,1,128]{2,0,1:T(8,128)(2,1)}, u32[]{:S(2)}) copy-start(bf16[512,1,128]{2,0,1:T(8,128)(2,1)} %get-tuple-element.1228) | copy-start | bytes 393220
  89.7 33.7 %reduce-scatter.5.cloned.1.call-start = ((), (), s32[]{:S(2)}) async-start(), calls=%async_computation.5 | async-start | bytes 786432 | tf_op jit(solution)/shard_map/reduce_scatter | solution.py:296
  101.0 7.4 %all-to-all-start.2 = ((bf16[128,2,1,1,128]{4,1,3,2,0:T(2,128)(2,1)}), bf16[128,2,1,1,128]{4,1,3,2,0:T(2,128)(2,1)S(1)}, u32[]{:S(2)}, u32[]{:S(2)}) async-start(bf16[128,2,1,1,128]{4,1,3,2,0:T(2,128)(2,1)} %copy.67), calls=%async_computation.3 | async-start | bytes 131072 | tf_op jit(solution)/shard_map/all_to_all | solution.py:317
Sparse Core Ops, SparseCore 0:
  89.8 8.1 reduce-scatter.6
  100.3 14.6 reduce-scatter.4
where the time goes:
time: 133 us; the launch traced here: 132 us
  blocking collectives  68.9 us (52%)
  between operations  15.7 us (12%)
  local copies, waits for them, and re-layouts  12.3 us (9%)
  starting transfers between devices  10.9 us (8%)
  matrix products  9.01 us (7%)
  other arithmetic  7.87 us (6%)
  loops' own time  5.55 us (4%)
  waiting for transfers between devices  1.65 us (1%)
    psum x1, blocking collectives, per_device(): lax.psum((self_squares, cross_squares), ('sec', 'tp'))  32.7 us
    all_gather x1, blocking collectives, per_device(): lax.all_gather(returned, 'tp', axis=3, tiled=True)  13.9 us
    all_gather x1, blocking collectives, per_device(): lax.all_gather(self_key, 'ctx', axis=0, tiled=True)  7.02 us
    all_gather x1, blocking collectives, per_device(): lax.all_gather(self_value, 'ctx', axis=0, tiled=True)  6.16 us
    all_gather x1, blocking collectives, per_device(): lax.all_gather(memory_keys, 'ctx', axis=0, tiled=True)  4.58 us
    all_gather x1, blocking collectives, per_device(): lax.all_gather(memory_values, 'ctx', axis=0, tiled=True)  4.58 us
    all_to_all x1, starting transfers between devices, per_device(): lax.all_to_all(own_heads(memory_key), 'sec', split_axis=1, concat_axis=0,...  4.26 us
    unnamed x19, local copies, waits for them, and re-layouts  3.39 us
  transfers between devices with their start and end apart: 5, of which 1 were waited for; matrix products, arithmetic and copies ran while one was open for 18% of the time, Pallas kernels for 0%

commit v1 on v0

--- a/solution.py
+++ b/solution.py
@@ -315,7 +315,42 @@
     )
     rounded = memory_sums.reshape(section_rows, 2, 1, 1, columns)
     returned = lax.all_to_all(rounded, "sec", split_axis=0, concat_axis=2, tiled=True)
-    complete = lax.all_gather(returned, "tp", axis=3, tiled=True).reshape(
+
+    def clear_notes_by_axis(sample):
+        bus_axis = "tp"
+        a_next, newest, step_out = (
+            lax.axis_size(bus_axis),
+            lax.axis_index(bus_axis),
+            sample.shape[3],
+        )
+        shelf = [k0 * a_next if nth == 3 else k0 for nth, k0 in enumerate(sample.shape)]
+        field_out = big = sample
+        idx = 1
+        parts_out = lax.dynamic_update_slice_in_dim(
+            jnp.zeros(shelf, sample.dtype), sample, newest * step_out, axis=3
+        )
+        while idx < a_next // 2 + 1:
+            field_out = lax.ppermute(
+                field_out,
+                axis_name=bus_axis,
+                perm=[(nth, (nth + 1) % a_next) for nth in range(a_next)],
+            )
+            parts_out = lax.dynamic_update_slice_in_dim(
+                parts_out, field_out, (newest - idx) % a_next * step_out, axis=3
+            )
+            if 2 * idx < a_next:
+                big = lax.ppermute(
+                    big,
+                    axis_name=bus_axis,
+                    perm=[(nth, (nth - 1) % a_next) for nth in range(a_next)],
+                )
+                parts_out = lax.dynamic_update_slice_in_dim(
+                    parts_out, big, (newest + idx) % a_next * step_out, axis=3
+                )
+            idx += 1
+        return parts_out
+
+    complete = clear_notes_by_axis(returned).reshape(
         memory_rows, 2, section_count * tensor_count * columns
     )
     return (

time: 133 us -> 137 us (1.030)
  local copies, waits for them, and re-layouts: 12.3 us -> 22.5 us
  blocking collectives: 68.9 us -> 61.6 us
    all_gather x1 -> x0, blocking collectives: 13.9 us -> none  [per_device(): lax.all_gather(returned, 'tp', axis=3, tiled=True)]
    dynamic_update_slice x0 -> x4, local copies, waits for them, and re-layouts: none -> 10.6 us  [the longest x2 5.29 us: clear_notes_by_axis(): lax.dynamic_update_slice_in_dim(parts_out, field_out, (newest - idx) % a_...]
    all_to_all x0 -> x1, blocking collectives: none -> 6.49 us  [per_device(): lax.all_to_all(rounded, 'sec', split_axis=0, concat_axis=2, tiled=True)]
    ppermute x0 -> x3, starting transfers between devices: none -> 3.88 us  [the longest x1 3.28 us: clear_notes_by_axis(): lax.ppermute(big, axis_name=bus_axis, perm=[(nth, (nth - 1) % a_next) for...]
    all_to_all x1 -> x0, starting transfers between devices: 3.28 us -> none  [per_device(): lax.all_to_all(rounded, 'sec', split_axis=0, concat_axis=2, tiled=True)]
    ppermute x0 -> x3, waiting for transfers between devices: none -> 2.43 us  [the longest x2 2.42 us: clear_notes_by_axis(): lax.ppermute(field_out, axis_name=bus_axis, perm=[(nth, (nth + 1) % a_nex...]
    all_to_all x1 -> x0, waiting for transfers between devices: 1.59 us -> none  [per_device(): lax.all_to_all(rounded, 'sec', split_axis=0, concat_axis=2, tiled=True)]
  transfers between devices with their start and end apart: 5 -> 7, of which waited for: 1 -> 1; matrix products, arithmetic and copies ran while one was open for 18% -> 25% of each run, Pallas kernels for 0% -> 0%
where the time goes in v1:
time: 137 us; the launch traced here: 136 us
  blocking collectives  61.6 us (45%)
  local copies, waits for them, and re-layouts  22.5 us (16%)
  between operations  15.7 us (11%)
  starting transfers between devices  11.5 us (8%)
  matrix products  8.99 us (7%)
  other arithmetic  7.87 us (6%)
  loops' own time  5.55 us (4%)
  waiting for transfers between devices  2.49 us (2%)
    psum x1, blocking collectives, per_device(): lax.psum((self_squares, cross_squares), ('sec', 'tp'))  32.7 us
    all_gather x1, blocking collectives, per_device(): lax.all_gather(self_key, 'ctx', axis=0, tiled=True)  7.02 us
    all_to_all x1, blocking collectives, per_device(): lax.all_to_all(rounded, 'sec', split_axis=0, concat_axis=2, tiled=True)  6.49 us
    all_gather x1, blocking collectives, per_device(): lax.all_gather(self_value, 'ctx', axis=0, tiled=True)  6.16 us
    dynamic_update_slice x2, local copies, waits for them, and re-layouts, clear_notes_by_axis(): lax.dynamic_update_slice_in_dim(parts_out, field_out, (newest - idx) % a_...  5.29 us
    all_gather x1, blocking collectives, per_device(): lax.all_gather(memory_values, 'ctx', axis=0, tiled=True)  4.58 us
    all_gather x1, blocking collectives, per_device(): lax.all_gather(memory_keys, 'ctx', axis=0, tiled=True)  4.58 us
    all_to_all x1, starting transfers between devices, per_device(): lax.all_to_all(own_heads(memory_key), 'sec', split_axis=1, concat_axis=0,...  4.26 us
  transfers between devices with their start and end apart: 7, of which 1 were waited for; matrix products, arithmetic and copies ran while one was open for 25% of the time, Pallas kernels for 0%

profile of v1, /device:TPU:0, one launch (start us, length us, event | category | flops | bytes accessed | tf_op | source)
XLA Modules:
  0.0 136.2 jit_solution(13335472457339134669)
XLA Ops:
  7.2 1.0 reshape.417
  8.3 0.6 copy.89
  8.9 4.3 %all-to-all-start.1 = ((bf16[32,4,128]{2,0,1:T(8,128)(2,1)}), bf16[32,4,128]{2,0,1:T(8,128)(2,1)S(1)}, u32[]{:S(2)}, u32[]{:S(2)}) async-start(bf16[32,4,128]{2,0,1:T(8,128)(2,1)} %bitcast.165), calls=%async_computation.1 | async-start | bytes 65536 | tf_op jit(solution)/shard_map/all_to_all | solution.py:239
  13.2 1.0 reshape.414
  14.2 0.7 select_reduce_fusion.3
  14.9 0.6 fusion.88
  15.6 7.0 %all_gather.13 = bf16[1024,128]{1,0:T(8,128)(2,1)S(1)} all-gather(bf16[512,128]{1,0:T(8,128)(2,1)} %param.22), channel_id=1, replica_groups=mesh['sec'=4,'ctx'=2,'tp'=4] {'ctx'}, dimensions={0}, use_global_device_ids=true | all-gather | bytes 393216 | tf_op jit(solution)/shard_map/all_gather | solution.py:221
  22.6 0.7 select_reduce_fusion.2
  23.3 0.6 fusion.86
  25.3 6.2 %all_gather.12 = bf16[1024,128]{1,0:T(8,128)(2,1)S(1)} all-gather(bf16[512,128]{1,0:T(8,128)(2,1)} %param.23), channel_id=1, replica_groups=mesh['sec'=4,'ctx'=2,'tp'=4] {'ctx'}, dimensions={0}, use_global_device_ids=true | all-gather | bytes 393216 | tf_op jit(solution)/shard_map/all_gather | solution.py:222
  31.4 2.2 %conditional.3 = (f32[1,512]{1,0:T(1,128)S(1)}, f32[1,512]{1,0:T(1,128)S(1)}) conditional(s32[]{:T(128)} %convert_element_type.106, (s32[1024]{0:T(1024)S(1)}, s32[512]{0:T(512)S(1)}, bf16[512,1,128]{2,0,1:T(8,128)(2,1)}, bf16[1024,128]{1,0:T(8,128)(2,1)S(1)}, f32[1,512]{1,0:T(1,128)S(1)}, /*index=5*/f32[1,512]{1,0:T(1,128)S(1)}) %tuple.182, ...), branch_computations={%region_4.7_spmd, %region_7.8_spmd} | conditional | flops 138937344 | bytes 4622352 | solution.py:62
  31.4 1.5 %fusion = (f32[512]{0:T(512)S(1)}, f32[512,1024]{1,0:T(8,128)S(1)}) fusion(s32[1024]{0:T(1024)S(1)} %get-tuple-element.800, s32[512]{0:T(512)S(1)} %get-tuple-element.801, bf16[1024,128]{1,0:T(8,128)(2,1)S(1)} %get-tuple-element.803, bf16[512,1,128]{2,0,1:T(8,128)(2,1)} %get-tuple-element.802), kind=kOutput, calls=%fused_computation.2 | convolution fusion | flops 136314368 | bytes 2498560 | tf_op jit(solution)/shard_map/while/body/eval_jaxpr/cond/branch_0_fun/qhd,khd->hqk/dot_general | solution.py:30
  32.9 0.7 exponential_reduce_fusion
  33.7 7.2 %while.24 = (s32[]{:T(128)}, f32[512,1,128]{0,2,1:T(8,128)S(1)}, s32[8]{0:T(128)S(1)}, s32[]{:T(128)}, bf16[1024,128]{1,0:T(8,128)(2,1)S(1)}, /*index=5*/s32[512...) while((s32[]{:T(128)}, f32[512,1,128]{0,2,1:T(8,128)S(1)}, ...), condition=%wide.region_13.14_spmd, body=%wide.region_8.13_spmd.sunk | while | flops 135621632 | bytes 935197 | solution.py:95
  33.8 0.6 fusion.107
  35.7 1.5 %conditional.6 = (f32[512,1,128]{0,2,1:T(8,128)S(1)}) conditional(s32[]{:T(128)} %convert_element_type.172, (s32[]{:T(128)}, bf16[1024,128]{1,0:T(8,128)(2,1)S(1)}, s32[512]{0:T(512)S(1)}, s32[512]{0:T(512)S(1)}, bf16[1024,128]{1,0:T(8,128)(2,1)S(1)}, /*index=5*/bf16[512,1,128]{2,0,1:T(8,128)(2,1)}, f32[1,512]{1,0:T(1,128)S(1)}, ...), branch_computations={%region_11.11_spmd, %region_12.12_spmd} | conditional | flops 135593984 | bytes 924714 | solution.py:91
  35.8 1.5 %fusion.10 = f32[512,1,128]{0,2,1:T(8,128)S(1)} fusion(f32[512,1,128]{0,2,1:T(8,128)S(1)} %get-tuple-element.807, f32[512]{0:T(512)S(1)} %bitcast.180, s32[512]{0:T(512)S(1)} %get-tuple-element.811, s32[512]{0:T(512)S(1)} %get-tuple-element.810, bf16[512,1,128]{2,0,1:T(8,128)(2,1)} %get-tuple-element.813, bf16[1024,128]{1,0:T(8,128)(2,1)S(1)} %get-tuple-element.812, ...), kind=kOutput, calls=%fused_computation.14 | convolution fusion | flops 135593984 | bytes 924672 | tf_op jit(solution)/shard_map/while/body/eval_jaxpr/cond/branch_0_fun/hqk,khd->qhd/dot_general | solution.py:85
  37.4 0.6 fusion.107
  39.3 1.5 %conditional.6 = (f32[512,1,128]{0,2,1:T(8,128)S(1)}) conditional(s32[]{:T(128)} %convert_element_type.172, (s32[]{:T(128)}, bf16[1024,128]{1,0:T(8,128)(2,1)S(1)}, s32[512]{0:T(512)S(1)}, s32[512]{0:T(512)S(1)}, bf16[1024,128]{1,0:T(8,128)(2,1)S(1)}, /*index=5*/bf16[512,1,128]{2,0,1:T(8,128)(2,1)}, f32[1,512]{1,0:T(1,128)S(1)}, ...), branch_computations={%region_11.11_spmd, %region_12.12_spmd} | conditional | flops 135593984 | bytes 924714 | solution.py:91
  39.3 1.5 %fusion.10 = f32[512,1,128]{0,2,1:T(8,128)S(1)} fusion(f32[512,1,128]{0,2,1:T(8,128)S(1)} %get-tuple-element.807, f32[512]{0:T(512)S(1)} %bitcast.180, s32[512]{0:T(512)S(1)} %get-tuple-element.811, s32[512]{0:T(512)S(1)} %get-tuple-element.810, bf16[512,1,128]{2,0,1:T(8,128)(2,1)} %get-tuple-element.813, bf16[1024,128]{1,0:T(8,128)(2,1)S(1)} %get-tuple-element.812, ...), kind=kOutput, calls=%fused_computation.14 | convolution fusion | flops 135593984 | bytes 924672 | tf_op jit(solution)/shard_map/while/body/eval_jaxpr/cond/branch_0_fun/hqk,khd->qhd/dot_general | solution.py:85
  41.0 0.2 fusion.64
  41.3 0.6 copy.90
  42.1 3.3 %all-to-all-start = ((bf16[32,4,128]{2,0,1:T(8,128)(2,1)}), bf16[32,4,128]{2,0,1:T(8,128)(2,1)S(1)}, u32[]{:S(2)}, u32[]{:S(2)}) async-start(bf16[32,4,128]{2,0,1:T(8,128)(2,1)} %bitcast.166), calls=%async_computation | async-start | bytes 65536 | tf_op jit(solution)/shard_map/all_to_all | solution.py:240
  45.4 4.6 %all_gather.15 = bf16[256,128]{1,0:T(8,128)(2,1)S(1)} all-gather(bf16[128,128]{1,0:T(8,128)(2,1)S(1)} %bitcast.174), channel_id=1, replica_groups=mesh['sec'=4,'ctx'=2,'tp'=4] {'ctx'}, dimensions={0}, use_global_device_ids=true | all-gather | bytes 98304 | tf_op jit(solution)/shard_map/all_gather | solution.py:250
  50.0 0.2 fusion.91
  50.4 4.6 %all_gather.14 = bf16[256,128]{1,0:T(8,128)(2,1)S(1)} all-gather(bf16[128,128]{1,0:T(8,128)(2,1)S(1)} %bitcast.175), channel_id=1, replica_groups=mesh['sec'=4,'ctx'=2,'tp'=4] {'ctx'}, dimensions={0}, use_global_device_ids=true | all-gather | bytes 98304 | tf_op jit(solution)/shard_map/all_gather | solution.py:251
  55.0 0.3 multiply_reduce_fusion.1
  55.2 32.7 %all-reduce = (f32[512]{0:T(512)S(1)}, f32[512]{0:T(512)S(1)}, f32[512]{0:T(512)S(1)}, f32[512]{0:T(512)S(1)}) all-reduce(f32[512]{0:T(512)S(1)} %get-tuple-element.924, f32[512]{0:T(512)S(1)} %get-tuple-element.922, f32[512]{0:T(512)S(1)} %get-tuple-element.923, ...), channel_id=1, replica_groups=mesh['sec'=4,'ctx'=2,'tp'=4] {'sec','tp'}, use_global_device_ids=true, to_apply=%region_15.16 | all-reduce | flops 2048 | bytes 16384 | tf_op jit(solution)/shard_map/psum | solution.py:265
  88.2 0.2 fusion.60
  88.4 0.2 fusion.56
  88.6 0.2 fusion.59
  88.9 0.8 copy.85
  89.7 0.9 fusion.68
  90.7 7.5 %while.25 = (s32[]{:T(128)}, f32[512,1,128]{0,2,1:T(8,128)S(1)}, bf16[1024,256]{0,1:T(8,128)(2,1)S(1)}, s32[8]{0:T(128)S(1)}, s32[]{:T(128)}, /*index=5*/bf16[10...) while((s32[]{:T(128)}, f32[512,1,128]{0,2,1:T(8,128)S(1)}, ...), condition=%wide.region_28.29_spmd, body=%wide.region_23.28_spmd.sunk | while | flops 338455552 | bytes 6965629 | solution.py:169
  90.8 0.6 fusion.108
  92.7 1.7 %conditional.7 = ((f32[512,1,128]{0,2,1:T(8,128)S(1)}, bf16[1024,256]{0,1:T(8,128)(2,1)S(1)})) conditional(s32[]{:T(128)} %convert_element_type.173, (s32[]{:T(128)}, bf16[1024,128]{1,0:T(8,128)(2,1)S(1)}, s32[512]{0:T(512)S(1)}, s32[512]{0:T(512)S(1)}, bf16[512,1,128]{2,0,1:T(8,128)(2,1)S(1)}, /*index=5*/f32[1,512]{1,0:T(1,128)S(1)}, ...), branch_computations={%region_26.26_spmd, %region_27.27_spmd} | conditional | flops 338427904 | bytes 6955082 | solution.py:161
  92.8 0.4 fusion.35
  93.1 0.3 fusion.36
  93.5 0.3 convolution_multiply_fusion.2
  93.8 0.3 fusion.39
  94.1 0.3 fusion.38
  94.5 0.6 fusion.108
  96.5 1.7 %conditional.7 = ((f32[512,1,128]{0,2,1:T(8,128)S(1)}, bf16[1024,256]{0,1:T(8,128)(2,1)S(1)})) conditional(s32[]{:T(128)} %convert_element_type.173, (s32[]{:T(128)}, bf16[1024,128]{1,0:T(8,128)(2,1)S(1)}, s32[512]{0:T(512)S(1)}, s32[512]{0:T(512)S(1)}, bf16[512,1,128]{2,0,1:T(8,128)(2,1)S(1)}, /*index=5*/f32[1,512]{1,0:T(1,128)S(1)}, ...), branch_computations={%region_26.26_spmd, %region_27.27_spmd} | conditional | flops 338427904 | bytes 6955082 | solution.py:161
  96.5 0.4 fusion.35
  96.9 0.3 fusion.36
  97.2 0.3 convolution_multiply_fusion.2
  97.5 0.3 fusion.39
  97.9 0.3 fusion.38
  98.2 1.0 copy.73
  99.2 0.9 copy.86
  100.3 6.5 %all_to_all.48 = bf16[128,2,1,1,128]{4,1,3,2,0:T(2,128)(2,1)S(1)} all-to-all(bf16[128,2,1,1,128]{4,1,3,2,0:T(2,128)(2,1)S(1)} %copy.76), channel_id=1, replica_groups=mesh['sec'=4,'ctx'=2,'tp'=4] {'sec'}, dimensions={0} | all-to-all | bytes 131072 | tf_op jit(solution)/shard_map/all_to_all | solution.py:317
  106.8 0.6 collective-permute-start
  107.4 3.3 %collective-permute-start.1 = (bf16[32,2,4,1,128]{4,0,3,2,1:T(8,128)(2,1)S(1)}, bf16[32,2,4,1,128]{4,0,3,2,1:T(8,128)(2,1)S(1)}, u32[]{:S(2)}, u32[]{:S(2)}) collective-permute-start(bf16[32,2,4,1,128]{4,0,3,2,1:T(8,128)(2,1)S(1)} %bitcast.170), channel_id=1, source_target_pairs={{0,3},{1,0},{2,1},{3,2},{4,7},{5,4},{6,5},{7,6},{8,11},{9,8},{10,9... | collective-permute-start | bytes 196616 | tf_op jit(solution)/shard_map/ppermute | solution.py:342
  110.7 2.4 %collective-permute-done = bf16[32,2,4,1,128]{4,0,3,2,1:T(8,128)(2,1)S(1)} collective-permute-done((bf16[32,2,4,1,128]{4,0,3,2,1:T(8,128)(2,1)S(1)}, bf16[32,2,4,1,128]{4,0,3,2,1:T(8,128)(2,1)S(1)}, u32[]{:S(2)}, u32[]{:S(2)}) %collective-permute-start) | collective-permute-done | bytes 65568 | tf_op jit(solution)/shard_map/ppermute | solution.py:333
  113.1 0.2 fusion.58
  113.4 0.8 copy.83
  114.1 0.8 copy.72
  114.9 0.8 copy.82
  115.8 2.6 %dynamic_update_slice.20 = bf16[32,2,4,4,128]{4,3,2,0,1:T(4,128)(2,1)S(1)} dynamic-update-slice(bf16[32,2,4,4,128]{4,3,2,0,1:T(4,128)(2,1)S(1)} %broadcast_in_dim.169, bf16[32,2,4,1,128]{4,3,2,0,1:T(2,128)(2,1)S(1)} %copy.78, s32[]{:T(128)} %constant.403.clone.1, s32[]{:T(128)} %constant.403.clone.1, s32[]{:T(128)} %constant.403.clone.1, s32[]{:T(128)S(6)} %select_n.222, s32[]{:T(128)} %constant.403.clone.1) | dynamic-update-slice | bytes 131076 | tf_op jit(solution)/shard_map/dynamic_update_slice | solution.py:329
  118.6 2.6 %dynamic_update_slice.21 = bf16[32,2,4,4,128]{4,3,2,0,1:T(4,128)(2,1)S(1)} dynamic-update-slice(bf16[32,2,4,4,128]{4,3,2,0,1:T(4,128)(2,1)S(1)} %dynamic_update_slice.20, bf16[32,2,4,1,128]{4,3,2,0,1:T(2,128)(2,1)S(1)} %copy.79, s32[]{:T(128)} %constant.403.clone.1, s32[]{:T(128)} %constant.403.clone.1, s32[]{:T(128)} %constant.403.clone.1, s32[]{:T(128)S(6)} %select_n.224, s32[]{:T(128)} %constant.403.clone.1) | dynamic-update-slice | bytes 131076 | tf_op jit(solution)/shard_map/dynamic_update_slice | solution.py:338
  121.4 2.6 %dynamic_update_slice.22 = bf16[32,2,4,4,128]{4,3,2,0,1:T(4,128)(2,1)S(1)} dynamic-update-slice(bf16[32,2,4,4,128]{4,3,2,0,1:T(4,128)(2,1)S(1)} %dynamic_update_slice.21, bf16[32,2,4,1,128]{4,3,2,0,1:T(2,128)(2,1)S(1)} %copy.80, s32[]{:T(128)} %constant.403.clone.1, s32[]{:T(128)} %constant.403.clone.1, s32[]{:T(128)} %constant.403.clone.1, s32[]{:T(128)S(6)} %select_n.226, s32[]{:T(128)} %constant.403.clone.1) | dynamic-update-slice | bytes 131076 | tf_op jit(solution)/shard_map/dynamic_update_slice | solution.py:347
  124.1 2.6 %dynamic_update_slice.23 = bf16[32,2,4,4,128]{4,3,2,0,1:T(4,128)(2,1)S(1)} dynamic-update-slice(bf16[32,2,4,4,128]{4,3,2,0,1:T(4,128)(2,1)S(1)} %dynamic_update_slice.22, bf16[32,2,4,1,128]{4,3,2,0,1:T(2,128)(2,1)S(1)} %copy.81, s32[]{:T(128)} %constant.403.clone.1, s32[]{:T(128)} %constant.403.clone.1, s32[]{:T(128)} %constant.403.clone.1, s32[]{:T(128)S(6)} %select_n.228, s32[]{:T(128)} %constant.403.clone.1) | dynamic-update-slice | bytes 131076 | tf_op jit(solution)/shard_map/dynamic_update_slice | solution.py:338
  127.0 0.7 slice_bitcast_fusion
  127.7 1.7 %fusion.90 = (bf16[512,128]{1,0:T(8,128)(2,1)}, bf16[512,128]{1,0:T(8,128)(2,1)}) fusion(bf16[512,256]{1,0:T(8,128)(2,1)} %reduce-scatter.5.cloned.1.call-done), kind=kLoop, calls=%fused_computation.160 | loop fusion | bytes 524288 | tf_op jit(solution)/shard_map/slice | solution.py:300
  (63 shorter events, 2.3 us)
Async XLA Ops:
  7.2 42.8 %copy-start = (bf16[512,128]{1,0:T(8,128)(2,1)S(1)}, bf16[512,128]{1,0:T(8,128)(2,1)}, u32[]{:S(2)}) copy-start(bf16[512,128]{1,0:T(8,128)(2,1)} %param.26) | copy-start | bytes 393220
  8.9 33.2 %all-to-all-start.1 = ((bf16[32,4,128]{2,0,1:T(8,128)(2,1)}), bf16[32,4,128]{2,0,1:T(8,128)(2,1)S(1)}, u32[]{:S(2)}, u32[]{:S(2)}) async-start(bf16[32,4,128]{2,0,1:T(8,128)(2,1)} %bitcast.165), calls=%async_computation.1 | async-start | bytes 65536 | tf_op jit(solution)/shard_map/all_to_all | solution.py:239
  31.4 2.2 %copy-start.4 = (s32[8]{0:T(128)S(1)}, s32[8]{0:T(128)}, u32[]{:S(2)}) copy-start(s32[8]{0:T(128)} %param.31) | copy-start | bytes 100
  33.6 7.4 %copy-start.2 = (bf16[512,128]{1,0:T(8,128)(2,1)S(1)}, bf16[512,128]{1,0:T(8,128)(2,1)}, u32[]{:S(2)}) copy-start(bf16[512,128]{1,0:T(8,128)(2,1)} %param.25) | copy-start | bytes 393220
  33.6 7.4 %copy-start.6 = (f32[128]{0:T(128)S(1)}, f32[128]{0:T(128)}, u32[]{:S(2)}) copy-start(f32[128]{0:T(128)} %param.24) | copy-start | bytes 1540
  33.7 8.3 %copy-start.3 = (bf16[512,128]{1,0:T(8,128)(2,1)S(1)}, bf16[512,128]{1,0:T(8,128)(2,1)}, u32[]{:S(2)}) copy-start(bf16[512,128]{1,0:T(8,128)(2,1)} %param.30) | copy-start | bytes 393220
  40.9 14.1 %copy-start.5 = (f32[128]{0:T(128)S(1)}, f32[128]{0:T(128)}, u32[]{:S(2)}) copy-start(f32[128]{0:T(128)} %param.29) | copy-start | bytes 1540
  42.1 8.3 %all-to-all-start = ((bf16[32,4,128]{2,0,1:T(8,128)(2,1)}), bf16[32,4,128]{2,0,1:T(8,128)(2,1)S(1)}, u32[]{:S(2)}, u32[]{:S(2)}) async-start(bf16[32,4,128]{2,0,1:T(8,128)(2,1)} %bitcast.166), calls=%async_computation | async-start | bytes 65536 | tf_op jit(solution)/shard_map/all_to_all | solution.py:240
  45.4 53.9 %reduce-scatter.7.cloned.1.call-start = ((), (), s32[]{:S(2)}) async-start(), calls=%async_computation.6 | async-start | bytes 196608
  88.1 2.5 %copy-start.1 = (bf16[512,1,128]{2,0,1:T(8,128)(2,1)S(1)}, bf16[512,1,128]{2,0,1:T(8,128)(2,1)}, u32[]{:S(2)}) copy-start(bf16[512,1,128]{2,0,1:T(8,128)(2,1)} %get-tuple-element.1228) | copy-start | bytes 393220
  89.7 38.0 %reduce-scatter.5.cloned.1.call-start = ((), (), s32[]{:S(2)}) async-start(), calls=%async_computation.5 | async-start | bytes 786432 | tf_op jit(solution)/shard_map/reduce_scatter | solution.py:296
  106.8 6.3 %collective-permute-start = (bf16[32,2,4,1,128]{4,0,3,2,1:T(8,128)(2,1)S(1)}, bf16[32,2,4,1,128]{4,0,3,2,1:T(8,128)(2,1)S(1)}, u32[]{:S(2)}, u32[]{:S(2)}) collective-permute-start(bf16[32,2,4,1,128]{4,0,3,2,1:T(8,128)(2,1)S(1)} %bitcast.169), channel_id=1, source_target_pairs={{0,1},{1,2},{2,3},{3,0},{4,5},{5,6},{6,7},{7,4},{8,9},{9,10},{10,1... | collective-permute-start | bytes 196616 | tf_op jit(solution)/shard_map/ppermute | solution.py:333
  107.4 13.8 %collective-permute-start.1 = (bf16[32,2,4,1,128]{4,0,3,2,1:T(8,128)(2,1)S(1)}, bf16[32,2,4,1,128]{4,0,3,2,1:T(8,128)(2,1)S(1)}, u32[]{:S(2)}, u32[]{:S(2)}) collective-permute-start(bf16[32,2,4,1,128]{4,0,3,2,1:T(8,128)(2,1)S(1)} %bitcast.170), channel_id=1, source_target_pairs={{0,3},{1,0},{2,1},{3,2},{4,7},{5,4},{6,5},{7,6},{8,11},{9,8},{10,9... | collective-permute-start | bytes 196616 | tf_op jit(solution)/shard_map/ppermute | solution.py:342
  113.1 10.9 %collective-permute-start.2 = (bf16[32,2,4,1,128]{4,0,3,2,1:T(8,128)(2,1)S(1)}, bf16[32,2,4,1,128]{4,0,3,2,1:T(8,128)(2,1)S(1)}, u32[]{:S(2)}, u32[]{:S(2)}) collective-permute-start(bf16[32,2,4,1,128]{4,0,3,2,1:T(8,128)(2,1)S(1)} %collective-permute-done), channel_id=1, source_target_pairs={{0,1},{1,2},{2,3},{3,0},{4,5},{5,6},{6,7},{7,4},{8,9},{9,10},{10,1... | collective-permute-start | bytes 196616 | tf_op jit(solution)/shard_map/ppermute | solution.py:333
Sparse Core Ops, SparseCore 0:
  89.8 8.1 reduce-scatter.6
  100.3 14.6 reduce-scatter.4
